TPU v7x, 32 devices: a whole 2x2x4 slice. The times are simulated.
32 devices in a mesh: dp: 8 (over z, x), ctx: 4 (over y, core).
Axes of the slice: x: 2, y: 2, z: 4, core: 2. Of those that a mesh axis runs over, the one named last changes fastest.
Arguments:
- features: bfloat16 [4096, 4096], P(('dp', 'ctx')), may hold values from -6 to 6
- gate_in: bfloat16 [4096, 4096], P(('dp', 'ctx')), may hold values from -6 to 6
- gate_out: bfloat16 [4096, 4096], P(('dp', 'ctx')), may hold values from -6 to 6
- value_weight: bfloat16 [4096, 4096], P('dp', 'ctx'), may hold values from -0.09375 to 0.09375
- short_taps: float32 [3, 7, 4096], replicated, may hold values from -2 to 2
- medium_taps: bfloat16 [128, 256], replicated, may hold values from -0.5 to 0.5
- cotangent: bfloat16 [4096, 4096], P(('dp', 'ctx')), may hold values from -6 to 6
Outputs:
- layer_out: bfloat16 [4096, 4096], P(('dp', 'ctx'))
- grad_features: bfloat16 [4096, 4096], P(('dp', 'ctx'))
- grad_gate_in: bfloat16 [4096, 4096], P(('dp', 'ctx'))
- grad_gate_out: bfloat16 [4096, 4096], P(('dp', 'ctx'))
- grad_weight: bfloat16 [4096, 4096], P('dp', 'ctx')
- grad_short: float32 [3, 7, 4096], P(None, None, 'ctx')
- grad_medium: float32 [128, 256], P(None, 'ctx')
All inputs are finite; a program needn't handle non-finite values.
Results may differ from a plain program's by a relative error of at most 0.025.
Values may be sent and summed in bfloat16 or wider, within the bound.
A program may use at most 256 MiB of HBM per device.

v0:
```python
import math
import jax
import jax.numpy as jnp
from jax import lax
from jax.sharding import PartitionSpec as P


def causal_conv(stream, conv_taps, prior_rows):
    conv_edge = conv_taps.shape[0] - 1
    row_count = stream.shape[0]
    extended = jnp.concatenate([prior_rows, stream], axis=0)
    running = conv_taps[0] * extended[conv_edge : conv_edge + row_count]
    for shift_back in range(1, conv_edge + 1):
        running = (
            running
            + conv_taps[shift_back]
            * extended[conv_edge - shift_back : conv_edge - shift_back + row_count]
        )
    return running


def conv_back(gradient, conv_taps, later_rows):
    conv_edge = conv_taps.shape[0] - 1
    row_count = gradient.shape[0]
    extended = jnp.concatenate([gradient, later_rows], axis=0)
    running = conv_taps[0] * extended[:row_count]
    for ahead in range(1, conv_edge + 1):
        running = running + conv_taps[ahead] * extended[ahead : ahead + row_count]
    return running


def conv_taps_grad(gradient, stream, prior_rows):
    conv_edge = prior_rows.shape[0]
    row_count = stream.shape[0]
    extended = jnp.concatenate([prior_rows, stream], axis=0)
    return jnp.stack(
        [
            jnp.sum(
                gradient * extended[conv_edge - shift_back : conv_edge - shift_back + row_count],
                axis=0,
            )
            for shift_back in range(conv_edge + 1)
        ]
    )


def toeplitz_table(medium):
    filter_span, group_count = medium.shape
    padded = jnp.concatenate(
        [
            jnp.zeros((1, group_count), medium.dtype),
            medium[::-1],
            jnp.zeros((filter_span, group_count), medium.dtype),
        ],
        axis=0,
    )
    tiled = jnp.tile(padded.T, (1, filter_span))
    return tiled[:, : 2 * filter_span * filter_span].reshape(
        group_count, filter_span, 2 * filter_span
    )


def fold_table(grad_table):
    group_count, filter_span, double_span = grad_table.shape
    flat = grad_table.reshape(group_count, filter_span * double_span)
    flat = jnp.concatenate([flat, jnp.zeros((group_count, filter_span), grad_table.dtype)], axis=1)
    summed = jnp.sum(flat.reshape(group_count, filter_span, double_span + 1), axis=1)
    return summed[:, 1 : filter_span + 1][:, ::-1].T


def apply_toeplitz(toeplitz, before, product):
    group_count, filter_span = (toeplitz.shape[0], toeplitz.shape[1])
    row_count, channels = product.shape
    block_shape = (row_count // filter_span, filter_span, group_count, channels // group_count)
    extended = jnp.concatenate([before, product], axis=0)
    lower_half = extended[:row_count].reshape(block_shape)
    upper_half = extended[filter_span:].reshape(block_shape)
    window = jnp.concatenate([lower_half, upper_half], axis=1)
    filtered = jnp.einsum("gij,bjgs->bigs", toeplitz, window, preferred_element_type=jnp.float32)
    return (filtered.reshape(row_count, channels), window)


def toeplitz_back(toeplitz, grad_filtered, later_rows, window):
    group_count, filter_span = (toeplitz.shape[0], toeplitz.shape[1])
    row_count, channels = grad_filtered.shape
    block_shape = (row_count // filter_span, filter_span, group_count, channels // group_count)
    current = grad_filtered.reshape(block_shape)
    following = jnp.concatenate([grad_filtered[filter_span:], later_rows], axis=0).reshape(
        block_shape
    )
    grad_product = jnp.einsum(
        "gij,bigs->bjgs", toeplitz[:, :, filter_span:], current, preferred_element_type=jnp.float32
    )
    grad_product = grad_product + jnp.einsum(
        "gij,bigs->bjgs",
        toeplitz[:, :, :filter_span],
        following,
        preferred_element_type=jnp.float32,
    )
    grad_table = jnp.einsum("bigs,bjgs->gij", current, window, preferred_element_type=jnp.float32)
    return (grad_product.reshape(row_count, channels), fold_table(grad_table))


def mixer_pass(
    stream_in,
    stream_out,
    stream_values,
    cot_rows,
    conv_taps,
    medium,
    fetch_rims,
    fetch_before,
    fetch_after,
    fetch_later,
):
    row_count = stream_in.shape[0]
    filter_span = medium.shape[0]
    conv_edge = conv_taps.shape[1] - 1
    streams = (stream_in, stream_out, stream_values)
    rims = fetch_rims(tuple((stream[row_count - conv_edge :] for stream in streams)))
    convs = [causal_conv(streams[index], conv_taps[index], rims[index]) for index in range(3)]
    product = (convs[0] * convs[2]).astype(jnp.bfloat16)
    toeplitz = toeplitz_table(medium)
    filtered, window = apply_toeplitz(
        toeplitz, fetch_before(product[row_count - filter_span :]), product
    )
    layer_out = (convs[1] * filtered).astype(jnp.bfloat16)
    grad_filtered = (cot_rows * convs[1]).astype(jnp.bfloat16)
    grad_product, medium_grad = toeplitz_back(
        toeplitz, grad_filtered, fetch_after(grad_filtered[:filter_span]), window
    )
    grad_convs = (grad_product * convs[2], cot_rows * filtered, grad_product * convs[0])
    later = fetch_later(tuple((gradient[:conv_edge] for gradient in grad_convs)))
    grad_streams = [
        conv_back(grad_convs[index], conv_taps[index], later[index]) for index in range(3)
    ]
    short_grad = jnp.stack(
        [conv_taps_grad(grad_convs[index], streams[index], rims[index]) for index in range(3)]
    )
    return (layer_out, grad_streams, short_grad, medium_grad)


def zero_tuple(tail_rows):
    return tuple((jnp.zeros_like(piece) for piece in tail_rows))


def local(features, gate_in, gate_out, value_weight, short_taps, medium_taps, cotangent):
    ctx_count = lax.axis_size("ctx")
    dp_count = lax.axis_size("dp")
    ctx_index = lax.axis_index("ctx")
    own_rows, channels = features.shape
    block_cols = value_weight.shape[1]
    group_count = medium_taps.shape[1]
    total_rows = own_rows * ctx_count * dp_count
    row_scale = 1.0 / math.sqrt(total_rows)
    group_scale = 1.0 / math.sqrt(total_rows * (channels // group_count))
    weight_block = lax.all_gather(value_weight, "dp", axis=0, tiled=True)
    feature_window = lax.all_gather(features, "ctx", axis=0, tiled=True)
    values_block = jnp.dot(feature_window, weight_block, preferred_element_type=jnp.float32).astype(
        jnp.bfloat16
    )
    block_in, block_out, block_cot = (
        lax.all_to_all(gate_in, "ctx", split_axis=1, concat_axis=0, tiled=True),
        lax.all_to_all(gate_out, "ctx", split_axis=1, concat_axis=0, tiled=True),
        lax.all_to_all(cotangent, "ctx", split_axis=1, concat_axis=0, tiled=True),
    )
    taps_block = lax.dynamic_slice_in_dim(short_taps, ctx_index * block_cols, block_cols, 2)
    group_block = group_count // ctx_count
    medium_block = lax.dynamic_slice_in_dim(medium_taps, ctx_index * group_block, group_block, 1)
    out_block, grad_streams, short_grad, medium_grad = mixer_pass(
        block_in,
        block_out,
        values_block,
        block_cot,
        taps_block,
        medium_block,
        zero_tuple,
        jnp.zeros_like,
        jnp.zeros_like,
        zero_tuple,
    )
    layer_out = lax.all_to_all(out_block, "ctx", split_axis=0, concat_axis=1, tiled=True)
    grad_gate_in, grad_gate_out = (
        lax.all_to_all(
            grad_streams[0].astype(jnp.bfloat16), "ctx", split_axis=0, concat_axis=1, tiled=True
        ),
        lax.all_to_all(
            grad_streams[1].astype(jnp.bfloat16), "ctx", split_axis=0, concat_axis=1, tiled=True
        ),
    )
    grad_values = grad_streams[2].astype(jnp.bfloat16)
    grad_short, grad_medium = (
        lax.psum((short_grad * row_scale).astype(jnp.bfloat16), "dp").astype(jnp.float32),
        lax.psum((medium_grad * group_scale).astype(jnp.bfloat16), "dp").astype(jnp.float32),
    )
    grad_weight = lax.psum_scatter(
        (
            lax.dot_general(
                feature_window,
                grad_values,
                (((0,), (0,)), ((), ())),
                preferred_element_type=jnp.float32,
            )
            * row_scale
        ).astype(jnp.bfloat16),
        "dp",
        scatter_dimension=0,
        tiled=True,
    )
    grad_features = lax.psum_scatter(
        lax.dot_general(
            grad_values, weight_block, (((1,), (1,)), ((), ())), preferred_element_type=jnp.float32
        ).astype(jnp.bfloat16),
        "ctx",
        scatter_dimension=0,
        tiled=True,
    )
    return (
        layer_out,
        grad_features,
        grad_gate_in,
        grad_gate_out,
        grad_weight,
        grad_short,
        grad_medium,
    )


def solution(mesh):
    in_specs = (
        P(("dp", "ctx"), None),
        P(("dp", "ctx"), None),
        P(("dp", "ctx"), None),
        P("dp", "ctx"),
        P(),
        P(),
        P(("dp", "ctx"), None),
    )
    out_specs = (
        P(("dp", "ctx"), None),
        P(("dp", "ctx"), None),
        P(("dp", "ctx"), None),
        P(("dp", "ctx"), None),
        P("dp", "ctx"),
        P(None, None, "ctx"),
        P(None, "ctx"),
    )
    return jax.shard_map(local, mesh=mesh, in_specs=in_specs, out_specs=out_specs, check_vma=False)
```

profile of v0, /device:TPU:0, one launch (start us, length us, event | category | flops | bytes accessed | tf_op | source)
XLA Modules:
  0.0 425.9 jit_solution(8969090850510553351)
XLA Ops:
  7.2 0.7 all-gather.3.cloned.1.call-update
  8.0 0.7 all-gather.5.cloned.1.call-update
  8.7 1.3 copy.44
  10.0 4.2 all-to-all-start
  14.2 1.3 copy.55
  15.5 19.7 %all-to-all-done = bf16[128,4,1024]{0,2,1:T(8,128)(2,1)S(1)} async-done(((bf16[128,4,1024]{0,2,1:T(8,128)(2,1)}), bf16[128,4,1024]{0,2,1:T(8,128)(2,1)S(1)}, u32[]{:S(2)}, u32[]{:S(2)}) %all-to-all-start) | async-done | bytes 1048608 | tf_op jit(solution)/shard_map/all_to_all | solution.py:164
  35.3 3.5 all-to-all-start.3
  39.3 3.2 tile.4
  42.5 10.9 %tile.10 = bf16[64,32896]{1,0:T(8,128)(2,1)} reshape(bf16[64,128,257]{2,1,0:T(8,128)(2,1)} %tile.4) | data formatting | bytes 8421376 | tf_op jit(solution)/shard_map/tile | solution.py:57
  53.3 2.2 slice-done
  55.5 3.1 copy.80
  58.6 1.1 copy.104
  59.7 1.6 constant_dynamic-slice_fusion.4
  61.3 1.3 copy.45
  62.6 3.5 all-to-all-start.1
  66.7 2.2 fusion.57
  68.9 1.9 copy.56
  70.8 6.7 %fusion.43 = (bf16[512,1024]{1,0:T(8,128)(2,1)S(1)}, f32[512,1024]{1,0:T(8,128)}) fusion(f32[4,128,1024]{2,1,0:T(8,128)S(1)} %copy.56, f32[1024]{0:T(1024)S(1)} %bitcast.192, f32[1024]{0:T(1024)S(1)} %bitcast.194, f32[1024]{0:T(1024)S(1)} %bitcast.196, f32[1024]{0:T(1024)S(1)} %bitcast.198, f32[1024]{0:T(1024)S(1)} %bitcast.200, ...), kind=kLoop, calls=%fused_computation.91 | loop fusion | flops 11534336 | bytes 6320128 | tf_op jit(solution)/shard_map/convert_element_type | solution.py:128
  77.5 1.0 copy-done.15
  78.5 2.3 copy.57
  81.5 1.4 reshape.119
  82.9 2.7 fusion.41
  86.2 0.7 add_bitcast_fusion
  86.9 1.0 copy.61
  87.9 1.5 copy.102
  89.4 1.9 copy.62
  91.3 97.8 %all-gather.5.cloned.1.call-done = bf16[4096,1024]{1,0:T(8,128)(2,1)} async-done(((bf16[512,1024]{1,0:T(8,128)(2,1)}), bf16[4096,1024]{1,0:T(8,128)(2,1)}) %all-gather.5.cloned.1.call-update) | async-done | bytes 8388624 | tf_op jit(solution)/shard_map/all_gather | solution.py:157
  189.1 10.1 %convolution_convert_fusion.1 = bf16[512,1024]{1,0:T(8,128)(2,1)} fusion(bf16[512,4096]{1,0:T(8,128)(2,1)} %all-gather.3.cloned.1.call-done, bf16[4096,1024]{1,0:T(8,128)(2,1)} %all-gather.5.cloned.1.call-done), kind=kOutput, calls=%fused_computation.102 | convolution fusion | flops 4295491584 | bytes 13631488 | tf_op jit(solution)/shard_map/dot_general | solution.py:159
  199.3 8.8 %fusion.27 = (f32[1024]{0:T(1024)S(1)}, f32[1024]{0:T(1024)S(1)}, f32[1024]{0:T(1024)S(1)}, f32[1024]{0:T(1024)S(1)}, f32[1024]{0:T(1024)S(1)}, /*index=5*/f32[1...) fusion(bf16[512,1024]{1,0:T(8,128)(2,1)S(1)} %bitcast.157, ...), kind=kLoop, calls=%fused_computation.69 | loop fusion | flops 22012928 | bytes 9494528 | tf_op jit(solution)/shard_map/reduce_sum | solution.py:38
  208.1 6.7 %fusion.40 = (f32[1024]{0:T(1024)S(1)}, f32[1024]{0:T(1024)S(1)}, f32[1024]{0:T(1024)S(1)}, f32[1024]{0:T(1024)S(1)}, f32[1024]{0:T(1024)S(1)}, /*index=5*/f32[1...) fusion(bf16[512,1024]{1,0:T(8,128)(2,1)S(1)} %copy-done.17, ...), kind=kLoop, calls=%fused_computation.82 | loop fusion | flops 29352960 | bytes 11591680 | tf_op jit(solution)/shard_map/reduce_sum | solution.py:38
  214.8 1.8 add_convert_fusion.2
  216.6 6.8 %fusion = bf16[4096,1024]{0,1:T(8,128)(2,1)} fusion(bf16[512,1024]{1,0:T(8,128)(2,1)S(1)} %add_convert_fusion.2, bf16[512,4096]{1,0:T(8,128)(2,1)S(1)} %copy-done.21), kind=kOutput, calls=%fused_computation.1 | convolution fusion | flops 4303355904 | bytes 13631488 | tf_op jit(solution)/shard_map/dot_general | solution.py:198
  223.5 9.5 %convolution_convert_fusion = bf16[512,4096]{1,0:T(8,128)(2,1)} fusion(bf16[512,1024]{1,0:T(8,128)(2,1)S(1)} %add_convert_fusion.2, bf16[4096,1024]{1,0:T(8,128)(2,1)} %all-gather.5.cloned.1.call-done), kind=kOutput, calls=%fused_computation.2 | convolution fusion | flops 4297064448 | bytes 13631488 | tf_op jit(solution)/shard_map/dot_general | solution.py:211
  232.9 1.6 copy-done.13
  234.5 1.9 multiply_convert_fusion.2
  236.4 1.3 copy.48
  238.4 1.1 reshape.115
  239.5 2.2 reshape.116
  241.8 1.7 copy_dynamic-update-slice_fusion.1
  243.4 1.7 copy_dynamic-update-slice_fusion
  245.1 1.7 fusion.44
  246.8 1.0 copy.52
  247.8 1.5 copy.103
  249.4 3.1 copy.53
  252.5 4.6 %fusion.14 = (f32[1024]{0:T(1024)S(1)}, f32[1024]{0:T(1024)S(1)}, f32[1024]{0:T(1024)S(1)}, f32[1024]{0:T(1024)S(1)}, f32[1024]{0:T(1024)S(1)}, /*index=5*/f32[1...) fusion(bf16[512,1024]{1,0:T(8,128)(2,1)S(1)} %bitcast.160, f32[512,1024]{1,0:T(8,128)} %copy.53, ...), kind=kLoop, calls=%fused_computation.56 | loop fusion | flops 11003904 | bytes 10510336 | tf_op jit(solution)/shard_map/reduce_sum | solution.py:38
  257.1 17.6 %all_to_all.108 = bf16[4,128,1024]{2,1,0:T(8,128)(2,1)} all-to-all(bf16[4,128,1024]{2,1,0:T(8,128)(2,1)S(1)} %bitcast.167), channel_id=1, replica_groups=mesh['dp'=8,'ctx'=4] {'ctx'}, dimensions={0} | all-to-all | bytes 2097152 | tf_op jit(solution)/shard_map/all_to_all | solution.py:182
  274.7 4.3 all-to-all-start.4
  279.0 8.3 %add_convert_fusion = bf16[512,1024]{1,0:T(8,128)(2,1)} fusion(f32[512,1024]{1,0:T(8,128)} %get-tuple-element.52, f32[1024]{0:T(1024)S(1)} %bitcast.193, f32[1024]{0:T(1024)S(1)} %bitcast.195, f32[1024]{0:T(1024)S(1)} %bitcast.197, f32[1024]{0:T(1024)S(1)} %bitcast.199, f32[1024]{0:T(1024)S(1)} %bitcast.201, f32[1024]{0:T(1024)S(1)} %bitcast.203, ...), kind=kLoop, calls=%fused_computation.95 | loop fusion | flops 7340032 | bytes 3174400 | tf_op jit(solution)/shard_map/convert_element_type | solution.py:188
  287.3 6.1 %all-to-all-done.4 = bf16[4,128,1024]{2,1,0:T(8,128)(2,1)} async-done(((bf16[4,128,1024]{2,1,0:T(8,128)(2,1)}), bf16[4,128,1024]{2,1,0:T(8,128)(2,1)}, u32[]{:S(2)}, u32[]{:S(2)}) %all-to-all-start.4) | async-done | bytes 1048608 | tf_op jit(solution)/shard_map/all_to_all | solution.py:184
  293.4 4.5 %all-to-all-start.5 = ((bf16[4,128,1024]{2,1,0:T(8,128)(2,1)}), bf16[4,128,1024]{2,1,0:T(8,128)(2,1)}, u32[]{:S(2)}, u32[]{:S(2)}) async-start(bf16[4,128,1024]{2,1,0:T(8,128)(2,1)} %bitcast.170), calls=%async_computation.6 | async-start | bytes 2097152 | tf_op jit(solution)/shard_map/all_to_all | solution.py:187
  297.9 1.3 fusion.49
  299.2 4.7 %copy.84 = f32[8,8,128,256]{3,1,2,0:T(8,128)S(1)} copy(f32[8,8,128,256]{3,2,1,0:T(8,128)S(1)} %bitcast.155) | data formatting | bytes 16777216
  304.0 3.9 concatenate.46
  307.9 14.3 %reshape.123 = f32[64,128,257]{2,1,0:T(8,128)} reshape(f32[64,32896]{1,0:T(8,128)} %concatenate.46) | data formatting | bytes 16842752 | tf_op jit(solution)/shard_map/reshape | solution.py:67
  322.2 6.3 %reduce_sum.219 = f32[64,257]{1,0:T(8,128)S(1)} reduce(f32[64,128,257]{2,1,0:T(8,128)} %reshape.123, f32[]{:T(128)} %constant.1.clone.1), dimensions={1}, to_apply=%region_24.0 | reduce | flops 2088896 | bytes 8487172 | tf_op jit(solution)/shard_map/reduce_sum | solution.py:67
  328.9 36.9 %all-reduce.9 = (bf16[3,7,1024]{2,1,0:T(8,128)(2,1)S(1)}, bf16[128,64]{0,1:T(8,128)(2,1)S(1)}) all-reduce(bf16[3,7,1024]{2,1,0:T(8,128)(2,1)S(1)} %fusion.52, bf16[128,64]{0,1:T(8,128)(2,1)S(1)} %fusion.53), channel_id=1, replica_groups=mesh['dp'=8,'ctx'=4] {'dp'}, use_global_device_ids=true, to_apply=%region_23.0 | all-reduce | flops 29696 | bytes 118784 | tf_op jit(solution)/shard_map/psum | solution.py:193
  365.8 0.6 convert_element_type.191
  367.1 0.7 copy.54
  367.7 1.3 copy.70
  369.0 2.3 copy.79
  371.3 1.6 copy.66
  373.0 1.3 copy.71
  374.3 2.3 copy.72
  376.6 42.6 %reduce-scatter.3.cloned.1.call-done = bf16[128,4096]{1,0:T(8,128)(2,1)} async-done(((bf16[512,4096]{1,0:T(8,128)(2,1)}), bf16[128,4096]{1,0:T(8,128)(2,1)}) %reduce-scatter.3.cloned.1.call-update) | async-done | bytes 1048592 | tf_op jit(solution)/shard_map/reduce_scatter | solution.py:210
  (76 shorter events, 4.2 us)
Async XLA Ops:
  7.2 31.6 %copy-start = (bf16[128,256]{1,0:T(8,128)(2,1)S(1)}, bf16[128,256]{1,0:T(8,128)(2,1)}, u32[]{:S(2)}) copy-start(bf16[128,256]{1,0:T(8,128)(2,1)} %param.12) | copy-start | bytes 196612
  7.2 1.5 copy-start.18
  7.2 84.1 %all-gather.3.cloned.1.call-start = ((), (), s32[]{:S(2)}) async-start(), calls=%async_computation.8 | async-start | bytes 5242880 | tf_op jit(solution)/shard_map/all_gather | solution.py:158
  7.9 181.2 %all-gather.5.cloned.1.call-start = ((), (), s32[]{:S(2)}) async-start(), calls=%async_computation.9 | async-start | bytes 9437184 | tf_op jit(solution)/shard_map/all_gather | solution.py:157
  8.7 5.6 %copy-start.19 = (bf16[128,4096]{1,0:T(8,128)(2,1)S(1)}, bf16[128,4096]{1,0:T(8,128)(2,1)}, u32[]{:S(2)}) copy-start(bf16[128,4096]{1,0:T(8,128)(2,1)} %param.13) | copy-start | bytes 3145732
  10.0 25.3 %all-to-all-start = ((bf16[128,4,1024]{0,2,1:T(8,128)(2,1)}), bf16[128,4,1024]{0,2,1:T(8,128)(2,1)S(1)}, u32[]{:S(2)}, u32[]{:S(2)}) async-start(bf16[128,4,1024]{0,2,1:T(8,128)(2,1)} %bitcast.1), calls=%async_computation | async-start | bytes 2097152 | tf_op jit(solution)/shard_map/all_to_all | solution.py:164
  35.3 26.0 %copy-start.11 = (bf16[128,4,1024]{0,2,1:T(8,128)(2,1)}, bf16[128,4,1024]{0,2,1:T(8,128)(2,1)S(1)}, u32[]{:S(2)}) copy-start(bf16[128,4,1024]{0,2,1:T(8,128)(2,1)S(1)} %all-to-all-done) | copy-start | bytes 3145732
  35.3 27.4 %all-to-all-start.3 = ((bf16[128,4,1024]{0,2,1:T(8,128)(2,1)}), bf16[128,4,1024]{0,2,1:T(8,128)(2,1)S(1)}, u32[]{:S(2)}, u32[]{:S(2)}) async-start(bf16[128,4,1024]{0,2,1:T(8,128)(2,1)} %bitcast.33), calls=%async_computation.3 | async-start | bytes 2097152 | tf_op jit(solution)/shard_map/all_to_all | solution.py:165
  53.3 2.2 slice-start
  55.5 3.1 copy-start.20
  62.6 136.6 %all-to-all-start.1 = ((bf16[128,4,1024]{2,0,1:T(8,128)(2,1)}), bf16[128,4,1024]{2,0,1:T(8,128)(2,1)S(1)}, u32[]{:S(2)}, u32[]{:S(2)}) async-start(bf16[128,4,1024]{2,0,1:T(8,128)(2,1)} %bitcast.169), calls=%async_computation.1 | async-start | bytes 2097152 | tf_op jit(solution)/shard_map/all_to_all | solution.py:163
  66.2 308.1 %reduce-scatter.5.cloned.1.call-start = ((), (), s32[]{:S(2)}) async-start(), calls=%async_computation.11 | async-start | bytes 9437184 | tf_op jit(solution)/shard_map/reduce_scatter | solution.py:196
  70.8 6.7 %copy-start.4 = (f32[4,128,1024]{2,1,0:T(8,128)}, f32[4,128,1024]{2,1,0:T(8,128)S(1)}, u32[]{:S(2)}) copy-start(f32[4,128,1024]{2,1,0:T(8,128)S(1)} %copy.56) | copy-start | bytes 6291460
  77.5 1.0 copy-start.15
  82.9 2.7 copy-start.9
  82.9 3.2 copy-start.2
  199.3 8.8 %copy-start.17 = (bf16[512,1024]{1,0:T(8,128)(2,1)S(1)}, bf16[512,1024]{1,0:T(8,128)(2,1)}, u32[]{:S(2)}) copy-start(bf16[512,1024]{1,0:T(8,128)(2,1)} %convolution_convert_fusion.1) | copy-start | bytes 3145732
  208.1 8.5 %copy-start.21 = (bf16[512,4096]{1,0:T(8,128)(2,1)S(1)}, bf16[512,4096]{1,0:T(8,128)(2,1)}, u32[]{:S(2)}) copy-start(bf16[512,4096]{1,0:T(8,128)(2,1)} %all-gather.3.cloned.1.call-done) | copy-start | bytes 12582916
  223.4 195.7 %reduce-scatter.3.cloned.1.call-start = ((), (), s32[]{:S(2)}) async-start(), calls=%async_computation.10 | async-start | bytes 5242880 | tf_op jit(solution)/shard_map/reduce_scatter | solution.py:210
  232.9 1.6 copy-start.13
  238.4 6.7 %copy-start.14 = (f32[128,4,1024]{0,2,1:T(8,128)S(1)}, f32[128,4,1024]{0,2,1:T(8,128)}, u32[]{:S(2)}) copy-start(f32[128,4,1024]{0,2,1:T(8,128)} %get-tuple-element.58) | copy-start | bytes 6291460
  239.5 5.6 %copy-start.12 = (bf16[128,4,1024]{0,2,1:T(8,128)(2,1)S(1)}, bf16[128,4,1024]{0,2,1:T(8,128)(2,1)}, u32[]{:S(2)}) copy-start(bf16[128,4,1024]{0,2,1:T(8,128)(2,1)} %copy-done.11) | copy-start | bytes 3145732
  241.8 3.4 copy-start.3
  245.1 1.8 copy-start.6
  249.4 3.1 copy-start.5
  249.4 3.1 copy-start.8
  274.7 18.8 %all-to-all-start.4 = ((bf16[4,128,1024]{2,1,0:T(8,128)(2,1)}), bf16[4,128,1024]{2,1,0:T(8,128)(2,1)}, u32[]{:S(2)}, u32[]{:S(2)}) async-start(bf16[4,128,1024]{2,1,0:T(8,128)(2,1)} %bitcast.41), calls=%async_computation.5 | async-start | bytes 2097152 | tf_op jit(solution)/shard_map/all_to_all | solution.py:184
  279.0 18.9 %copy-start.7 = (bf16[4,256,64,16]{1,3,0,2:T(8,128)(2,1)S(1)}, bf16[4,256,64,16]{1,3,0,2:T(8,128)(2,1)}, u32[]{:S(2)}) copy-start(bf16[4,256,64,16]{1,3,0,2:T(8,128)(2,1)} %copy-done.6) | copy-start | bytes 6291460
  279.0 18.9 %copy-start.10 = (bf16[4,128,64,16]{1,0,3,2:T(4,128)(2,1)S(1)}, bf16[4,128,64,16]{1,0,3,2:T(4,128)(2,1)}, u32[]{:S(2)}) copy-start(bf16[4,128,64,16]{1,0,3,2:T(4,128)(2,1)} %copy-done.9) | copy-start | bytes 3145732
  293.4 77.9 %all-to-all-start.5 = ((bf16[4,128,1024]{2,1,0:T(8,128)(2,1)}), bf16[4,128,1024]{2,1,0:T(8,128)(2,1)}, u32[]{:S(2)}, u32[]{:S(2)}) async-start(bf16[4,128,1024]{2,1,0:T(8,128)(2,1)} %bitcast.170), calls=%async_computation.6 | async-start | bytes 2097152 | tf_op jit(solution)/shard_map/all_to_all | solution.py:187
  322.2 44.9 %copy-start.16 = (bf16[4,128,1024]{2,1,0:T(8,128)(2,1)S(1)}, bf16[4,128,1024]{2,1,0:T(8,128)(2,1)}, u32[]{:S(2)}) copy-start(bf16[4,128,1024]{2,1,0:T(8,128)(2,1)} %all_to_all.108) | copy-start | bytes 3145732
  373.0 46.2 %copy-start.1 = (bf16[128,256]{1,0:T(8,128)(2,1)S(1)}, bf16[128,256]{1,0:T(8,128)(2,1)}, u32[]{:S(2)}) copy-start(bf16[128,256]{1,0:T(8,128)(2,1)} %param.12) | copy-start | bytes 196612
Sparse Core Ops, SparseCore 0:
  9.6 52.1 all-gather.2
  63.9 125.1 all-gather.4
  223.5 148.3 reduce-scatter.4
  375.1 44.0 reduce-scatter.2
where the time goes:
time: 431 us; the launch traced here: 426 us
  waiting for transfers between devices  168 us (39%)
  local copies, waits for them, and re-layouts  87.2 us (20%)
  blocking collectives  54.5 us (13%)
  other arithmetic  48.7 us (11%)
  matrix products  32.8 us (8%)
  starting transfers between devices  20.6 us (5%)
  between operations  14.4 us (3%)
    all_gather x1, waiting for transfers between devices, local(): weight_block = lax.all_gather(value_weight, 'dp', axis=0, tiled=True)  97.8 us
    reduce_scatter x1, waiting for transfers between devices, local(): lax.psum_scatter(lax.dot_general(grad_values, weight_block, (((1,), (1,))...  42.6 us
    psum x1, blocking collectives, local(): lax.psum((short_grad * row_scale).astype(jnp.bfloat16), 'dp')  36.9 us
    unnamed x55, local copies, waits for them, and re-layouts  23.5 us
    reduce_sum x3, other arithmetic, conv_taps_grad(): jnp.sum(gradient * extended[conv_edge - shift_back:conv_edge - shift_back...  20.1 us
    all_to_all x1, waiting for transfers between devices, local(): lax.all_to_all(gate_out, 'ctx', split_axis=1, concat_axis=0, tiled=True)  19.7 us
    all_to_all x1, blocking collectives, local(): lax.all_to_all(out_block, 'ctx', split_axis=0, concat_axis=1, tiled=True)  17.6 us
    reshape x1, local copies, waits for them, and re-layouts, fold_table(): flat.reshape(group_count, filter_span, double_span + 1)  14.3 us
  transfers between devices with their start and end apart: 9, of which 4 were waited for; matrix products, arithmetic and copies ran while one was open for 33% of the time, Pallas kernels for 0%

commit v1 on v0

--- a/solution.py
+++ b/solution.py
@@ -3,6 +3,22 @@
 import jax.numpy as jnp
 from jax import lax
 from jax.sharding import PartitionSpec as P
+
+
+def pairwise_exchange(shard, axis, split, join):
+    ways, here = (lax.axis_size(axis), lax.axis_index(axis))
+    width = shard.shape[split] // ways
+    shape = list(shard.shape)
+    shape[split] = width
+    height = shape[join]
+    shape[join] = height * ways
+    full = jnp.zeros(shape, shard.dtype)
+    for mask in range(ways):
+        part = lax.dynamic_slice_in_dim(shard, (here ^ mask) * width, width, axis=split)
+        if mask:
+            part = lax.ppermute(part, axis, [(d, d ^ mask) for d in range(ways)])
+        full = lax.dynamic_update_slice_in_dim(full, part, (here ^ mask) * height, axis=join)
+    return full
 
 
 def causal_conv(stream, conv_taps, prior_rows):
@@ -179,7 +195,7 @@
         jnp.zeros_like,
         zero_tuple,
     )
-    layer_out = lax.all_to_all(out_block, "ctx", split_axis=0, concat_axis=1, tiled=True)
+    layer_out = pairwise_exchange(out_block, "ctx", 0, 1)
     grad_gate_in, grad_gate_out = (
         lax.all_to_all(
             grad_streams[0].astype(jnp.bfloat16), "ctx", split_axis=0, concat_axis=1, tiled=True

time: 431 us -> 431 us (level)
  waiting for transfers between devices: 168 us -> 195 us
  blocking collectives: 54.5 us -> 35.2 us
  local copies, waits for them, and re-layouts: 87.2 us -> 80.1 us
    reduce_scatter x1, waiting for transfers between devices: 0.01 us -> 27.2 us  [local(): lax.psum_scatter((lax.dot_general(feature_window, grad_values, (((0,), (0...]
    all_to_all x1 -> x0, blocking collectives: 17.6 us -> none  [local(): lax.all_to_all(out_block, 'ctx', split_axis=0, concat_axis=1, tiled=True)]
    convert_element_type x1 -> x0, other arithmetic: 8.33 us -> none  [local(): grad_streams[1].astype(jnp.bfloat16)]
    all_to_all x1, waiting for transfers between devices: 6.1 us -> 0.01 us  [local(): lax.all_to_all(grad_streams[0].astype(jnp.bfloat16), 'ctx', split_axis=0,...]
    all_to_all x0 -> x1, other arithmetic: none -> 5.21 us  [local(): lax.all_to_all(grad_streams[1].astype(jnp.bfloat16), 'ctx', split_axis=0,...]
    unnamed x55 -> x66, local copies, waits for them, and re-layouts: 23.5 us -> 21.2 us
  transfers between devices with their start and end apart: 9 -> 12, of which waited for: 4 -> 5; matrix products, arithmetic and copies ran while one was open for 33% -> 30% of each run, Pallas kernels for 0% -> 0%
where the time goes in v1:
time: 431 us; the launch traced here: 425 us
  waiting for transfers between devices  195 us (45%)
  local copies, waits for them, and re-layouts  80.1 us (19%)
  other arithmetic  44.6 us (10%)
  blocking collectives  35.2 us (8%)
  matrix products  34.5 us (8%)
  starting transfers between devices  21.3 us (5%)
  between operations  14.6 us (3%)
    all_gather x1, waiting for transfers between devices, local(): weight_block = lax.all_gather(value_weight, 'dp', axis=0, tiled=True)  101 us
    reduce_scatter x1, waiting for transfers between devices, local(): lax.psum_scatter(lax.dot_general(grad_values, weight_block, (((1,), (1,))...  44.4 us
    psum x1, blocking collectives, local(): lax.psum((short_grad * row_scale).astype(jnp.bfloat16), 'dp')  35.2 us
    reduce_scatter x1, waiting for transfers between devices, local(): lax.psum_scatter((lax.dot_general(feature_window, grad_values, (((0,), (0...  27.2 us
    unnamed x66, local copies, waits for them, and re-layouts  21.2 us
    reduce_sum x3, other arithmetic, conv_taps_grad(): jnp.sum(gradient * extended[conv_edge - shift_back:conv_edge - shift_back...  20.4 us
    all_to_all x1, waiting for transfers between devices, local(): lax.all_to_all(gate_out, 'ctx', split_axis=1, concat_axis=0, tiled=True)  19.7 us
    reshape x1, local copies, waits for them, and re-layouts, fold_table(): flat.reshape(group_count, filter_span, double_span + 1)  14.2 us
  transfers between devices with their start and end apart: 12, of which 5 were waited for; matrix products, arithmetic and copies ran while one was open for 30% of the time, Pallas kernels for 0%

profile of v1, /device:TPU:0, one launch (start us, length us, event | category | flops | bytes accessed | tf_op | source)
XLA Modules:
  0.0 425.5 jit_solution(13932080816840971028)
XLA Ops:
  7.2 0.7 all-gather.3.cloned.1.call-update
  8.0 0.7 all-gather.5.cloned.1.call-update
  8.7 1.3 copy.52
  10.0 4.2 all-to-all-start
  14.2 1.3 copy.65
  15.5 19.7 %all-to-all-done = bf16[128,4,1024]{0,2,1:T(8,128)(2,1)S(1)} async-done(((bf16[128,4,1024]{0,2,1:T(8,128)(2,1)}), bf16[128,4,1024]{0,2,1:T(8,128)(2,1)S(1)}, u32[]{:S(2)}, u32[]{:S(2)}) %all-to-all-start) | async-done | bytes 1048608 | tf_op jit(solution)/shard_map/all_to_all | solution.py:180
  35.3 3.5 all-to-all-start.2
  39.3 3.2 tile.4
  42.5 10.9 %tile.10 = bf16[64,32896]{1,0:T(8,128)(2,1)} reshape(bf16[64,128,257]{2,1,0:T(8,128)(2,1)} %tile.4) | data formatting | bytes 8421376 | tf_op jit(solution)/shard_map/tile | solution.py:73
  53.3 2.2 slice-done
  55.5 3.2 copy.88
  58.7 1.1 copy.118
  59.8 1.4 constant_dynamic-slice_fusion.4
  61.3 1.1 all-to-all-done.2
  62.4 1.0 copy-done.15
  63.4 3.5 all-to-all-start.1
  67.0 2.8 fusion.72
  69.8 4.8 %fusion.55 = (bf16[512,1024]{0,1:T(8,128)(2,1)S(1)}, f32[512,1024]{0,1:T(8,128)}) fusion(f32[4,128,8,128]{3,2,1,0:T(8,128)S(1)} %get-tuple-element.59, f32[1024]{0:T(1024)S(1)} %bitcast.195, f32[1024]{0:T(1024)S(1)} %bitcast.197, f32[1024]{0:T(1024)S(1)} %bitcast.199, f32[1024]{0:T(1024)S(1)} %bitcast.201, f32[1024]{0:T(1024)S(1)} %bitcast.203, ...), kind=kLoop, calls=%fused_computation.107 | loop fusion | flops 11534336 | bytes 6320128 | tf_op jit(solution)/shard_map/convert_element_type | solution.py:144
  74.5 1.0 slice.341
  75.8 2.6 concatenate.42
  78.3 1.3 reshape.117
  79.7 2.4 fusion.56
  82.5 0.7 add_bitcast_fusion
  83.3 1.0 copy.69
  84.2 1.5 copy.117
  85.7 1.9 copy.70
  87.7 101.5 %all-gather.5.cloned.1.call-done = bf16[4096,1024]{1,0:T(8,128)(2,1)} async-done(((bf16[512,1024]{1,0:T(8,128)(2,1)}), bf16[4096,1024]{1,0:T(8,128)(2,1)}) %all-gather.5.cloned.1.call-update) | async-done | bytes 8388624 | tf_op jit(solution)/shard_map/all_gather | solution.py:173
  189.1 10.1 %convolution_convert_fusion.1 = bf16[512,1024]{1,0:T(8,128)(2,1)} fusion(bf16[512,4096]{1,0:T(8,128)(2,1)} %all-gather.3.cloned.1.call-done, bf16[4096,1024]{1,0:T(8,128)(2,1)} %all-gather.5.cloned.1.call-done), kind=kOutput, calls=%fused_computation.120 | convolution fusion | flops 4295491584 | bytes 13631488 | tf_op jit(solution)/shard_map/dot_general | solution.py:175
  199.3 8.6 %fusion.27 = (f32[1024]{0:T(1024)S(1)}, f32[1024]{0:T(1024)S(1)}, f32[1024]{0:T(1024)S(1)}, f32[1024]{0:T(1024)S(1)}, f32[1024]{0:T(1024)S(1)}, /*index=5*/f32[1...) fusion(bf16[512,1024]{1,0:T(8,128)(2,1)S(1)} %bitcast.167, ...), kind=kLoop, calls=%fused_computation.75 | loop fusion | flops 22012928 | bytes 9494528 | tf_op jit(solution)/shard_map/reduce_sum | solution.py:54
  207.9 6.5 %fusion.40 = (f32[1024]{0:T(1024)S(1)}, f32[1024]{0:T(1024)S(1)}, f32[1024]{0:T(1024)S(1)}, f32[1024]{0:T(1024)S(1)}, f32[1024]{0:T(1024)S(1)}, /*index=5*/f32[1...) fusion(bf16[512,1024]{1,0:T(8,128)(2,1)S(1)} %copy-done.16, ...), kind=kLoop, calls=%fused_computation.88 | loop fusion | flops 29352960 | bytes 11591680 | tf_op jit(solution)/shard_map/reduce_sum | solution.py:54
  214.5 1.8 add_convert_fusion.1
  216.2 7.0 %fusion = bf16[4096,1024]{0,1:T(8,128)(2,1)} fusion(bf16[512,1024]{1,0:T(8,128)(2,1)S(1)} %add_convert_fusion.1, bf16[512,4096]{1,0:T(8,128)(2,1)S(1)} %copy-done.28), kind=kOutput, calls=%fused_computation.1 | convolution fusion | flops 4303355904 | bytes 13631488 | tf_op jit(solution)/shard_map/dot_general | solution.py:214
  223.3 9.5 %convolution_convert_fusion = bf16[512,4096]{1,0:T(8,128)(2,1)} fusion(bf16[512,1024]{1,0:T(8,128)(2,1)S(1)} %add_convert_fusion.1, bf16[4096,1024]{1,0:T(8,128)(2,1)} %all-gather.5.cloned.1.call-done), kind=kOutput, calls=%fused_computation.2 | convolution fusion | flops 4297064448 | bytes 13631488 | tf_op jit(solution)/shard_map/dot_general | solution.py:227
  232.8 1.5 copy-done.12
  234.4 1.9 multiply_convert_fusion.1
  237.5 1.1 reshape.112
  238.6 1.1 reshape.113
  239.7 1.6 copy_dynamic-update-slice_fusion.1
  241.3 1.7 copy_dynamic-update-slice_fusion
  243.0 3.5 fusion.58
  246.5 1.0 copy.60
  247.5 0.7 copy-done.5
  248.5 5.2 %fusion.14 = (f32[1024]{0:T(1024)}, f32[1024]{0:T(1024)}, f32[1024]{0:T(1024)}, f32[1024]{0:T(1024)}, f32[1024]{0:T(1024)}, /*index=5*/f32[1024]{0:T(1024)}, f32[512,1024]{0,1:T(8,128)}, bf16[512,1024]{0,1:T(8,128)(2,1)S(1)}) fusion(bf16[512,1024]{0,1:T(8,128)(2,1)S(1)} %copy-done.7, f32[128,8,4,128]{3,2,1,0:T(4,128)S(1)} %bitcast.172, ...), kind=kLoop, calls=%fused_computation.62 | loop fusion | flops 11003904 | bytes 10510336 | tf_op jit(solution)/shard_map/reduce_sum | solution.py:54
  253.7 1.0 constant_dynamic-slice_fusion.8
  254.7 1.5 collective-permute-start.1
  256.5 4.5 %all-to-all-start.3 = ((bf16[4,128,1024]{2,1,0:T(8,128)(2,1)}), bf16[4,128,1024]{2,1,0:T(8,128)(2,1)}, u32[]{:S(2)}, u32[]{:S(2)}) async-start(bf16[4,128,1024]{2,1,0:T(8,128)(2,1)} %bitcast.173), calls=%async_computation.4 | async-start | bytes 2097152 | tf_op jit(solution)/shard_map/all_to_all | solution.py:200
  261.0 1.3 fusion.64
  262.3 4.7 %copy.92 = f32[8,8,128,256]{3,1,2,0:T(8,128)S(1)} copy(f32[8,8,128,256]{3,2,1,0:T(8,128)S(1)} %bitcast.165) | data formatting | bytes 16777216
  267.1 3.8 concatenate.46
  270.9 14.2 %reshape.120 = f32[64,128,257]{2,1,0:T(8,128)} reshape(f32[64,32896]{1,0:T(8,128)} %concatenate.46) | data formatting | bytes 16842752 | tf_op jit(solution)/shard_map/reshape | solution.py:83
  285.1 6.3 %reduce_sum.219 = f32[64,257]{1,0:T(8,128)S(1)} reduce(f32[64,128,257]{2,1,0:T(8,128)} %reshape.120, f32[]{:T(128)} %constant.5.clone.1), dimensions={1}, to_apply=%region_24.0 | reduce | flops 2088896 | bytes 8487172 | tf_op jit(solution)/shard_map/reduce_sum | solution.py:83
  291.6 5.2 %copy_bitcast_fusion.2 = bf16[4,128,1024]{1,2,0:T(8,128)(2,1)} fusion(f32[512,1024]{0,1:T(8,128)S(1)} %copy-done.14, f32[1024]{0:T(1024)S(1)} %bitcast.196, f32[1024]{0:T(1024)S(1)} %bitcast.198, f32[1024]{0:T(1024)S(1)} %bitcast.200, f32[1024]{0:T(1024)S(1)} %bitcast.202, f32[1024]{0:T(1024)S(1)} %bitcast.204, f32[1024]{0:T(1024)S(1)} %bitcast.206, ...), kind=kLoop, calls=%fused_computation.129 | loop fusion | flops 7340032 | bytes 3174400 | tf_op jit(solution)/shard_map/all_to_all | solution.py:203
  296.8 3.5 all-to-all-start.4
  300.9 35.2 %all-reduce.9 = (bf16[3,7,1024]{2,1,0:T(8,128)(2,1)S(1)}, bf16[128,64]{0,1:T(8,128)(2,1)S(1)}) all-reduce(bf16[3,7,1024]{2,1,0:T(8,128)(2,1)S(1)} %fusion.67, bf16[128,64]{0,1:T(8,128)(2,1)S(1)} %fusion.68), channel_id=1, replica_groups=mesh['dp'=8,'ctx'=4] {'dp'}, use_global_device_ids=true, to_apply=%region_23.0 | all-reduce | flops 29696 | bytes 118784 | tf_op jit(solution)/shard_map/psum | solution.py:209
  336.1 0.6 convert_element_type.191
  336.7 0.6 convert_element_type.194
  337.5 1.1 copy.62
  338.6 1.1 copy.63
  339.7 1.1 copy.64
  340.9 2.7 copy.87
  343.6 1.3 copy.77
  344.9 27.2 %reduce-scatter.5.cloned.1.call-done = bf16[512,1024]{0,1:T(8,128)(2,1)} async-done(((bf16[4096,1024]{0,1:T(8,128)(2,1)}), bf16[512,1024]{0,1:T(8,128)(2,1)}) %reduce-scatter.5.cloned.1.call-update) | async-done | bytes 1048592 | tf_op jit(solution)/shard_map/reduce_scatter | solution.py:212
  372.1 2.3 copy.78
  374.3 44.4 %reduce-scatter.3.cloned.1.call-done = bf16[128,4096]{1,0:T(8,128)(2,1)} async-done(((bf16[512,4096]{1,0:T(8,128)(2,1)}), bf16[128,4096]{1,0:T(8,128)(2,1)}) %reduce-scatter.3.cloned.1.call-update) | async-done | bytes 1048592 | tf_op jit(solution)/shard_map/reduce_scatter | solution.py:226
  (97 shorter events, 4.2 us)
Async XLA Ops:
  7.2 31.6 %copy-start = (bf16[128,256]{1,0:T(8,128)(2,1)S(1)}, bf16[128,256]{1,0:T(8,128)(2,1)}, u32[]{:S(2)}) copy-start(bf16[128,256]{1,0:T(8,128)(2,1)} %param.12) | copy-start | bytes 196612
  7.2 1.5 copy-start.17
  7.2 80.5 %all-gather.3.cloned.1.call-start = ((), (), s32[]{:S(2)}) async-start(), calls=%async_computation.7 | async-start | bytes 5242880 | tf_op jit(solution)/shard_map/all_gather | solution.py:174
  7.9 181.2 %all-gather.5.cloned.1.call-start = ((), (), s32[]{:S(2)}) async-start(), calls=%async_computation.8 | async-start | bytes 9437184 | tf_op jit(solution)/shard_map/all_gather | solution.py:173
  8.7 5.6 %copy-start.18 = (bf16[128,4096]{1,0:T(8,128)(2,1)S(1)}, bf16[128,4096]{1,0:T(8,128)(2,1)}, u32[]{:S(2)}) copy-start(bf16[128,4096]{1,0:T(8,128)(2,1)} %param.13) | copy-start | bytes 3145732
  10.0 25.3 %all-to-all-start = ((bf16[128,4,1024]{0,2,1:T(8,128)(2,1)}), bf16[128,4,1024]{0,2,1:T(8,128)(2,1)S(1)}, u32[]{:S(2)}, u32[]{:S(2)}) async-start(bf16[128,4,1024]{0,2,1:T(8,128)(2,1)} %bitcast.1), calls=%async_computation | async-start | bytes 2097152 | tf_op jit(solution)/shard_map/all_to_all | solution.py:180
  35.3 25.9 %copy-start.10 = (bf16[128,4,1024]{0,2,1:T(8,128)(2,1)}, bf16[128,4,1024]{0,2,1:T(8,128)(2,1)S(1)}, u32[]{:S(2)}) copy-start(bf16[128,4,1024]{0,2,1:T(8,128)(2,1)S(1)} %all-to-all-done) | copy-start | bytes 3145732
  35.3 27.1 %all-to-all-start.2 = ((bf16[128,4,1024]{0,2,1:T(8,128)(2,1)}), bf16[128,4,1024]{0,2,1:T(8,128)(2,1)S(1)}, u32[]{:S(2)}, u32[]{:S(2)}) async-start(bf16[128,4,1024]{0,2,1:T(8,128)(2,1)} %bitcast.29), calls=%async_computation.2 | async-start | bytes 2097152 | tf_op jit(solution)/shard_map/all_to_all | solution.py:181
  53.3 2.2 slice-start
  55.5 3.2 copy-start.19
  61.3 8.4 %copy-start.6 = (bf16[512,1024]{0,1:T(8,128)(2,1)}, bf16[512,1024]{0,1:T(8,128)(2,1)S(1)}, u32[]{:S(2)}) copy-start(bf16[512,1024]{0,1:T(8,128)(2,1)S(1)} %copy_bitcast_fusion.1) | copy-start | bytes 3145732
  62.4 1.0 copy-start.15
  63.4 135.9 %all-to-all-start.1 = ((bf16[128,4,1024]{2,0,1:T(8,128)(2,1)}), bf16[128,4,1024]{2,0,1:T(8,128)(2,1)S(1)}, u32[]{:S(2)}, u32[]{:S(2)}) async-start(bf16[128,4,1024]{2,0,1:T(8,128)(2,1)} %bitcast.175), calls=%async_computation.1 | async-start | bytes 2097152 | tf_op jit(solution)/shard_map/all_to_all | solution.py:179
  66.9 305.2 %reduce-scatter.5.cloned.1.call-start = ((), (), s32[]{:S(2)}) async-start(), calls=%async_computation.10 | async-start | bytes 9437184 | tf_op jit(solution)/shard_map/reduce_scatter | solution.py:212
  69.7 4.8 %copy-start.4 = (f32[4,128,8,128]{3,2,1,0:T(8,128)}, f32[4,128,8,128]{3,2,1,0:T(8,128)S(1)}, u32[]{:S(2)}) copy-start(f32[4,128,8,128]{3,2,1,0:T(8,128)S(1)} %get-tuple-element.59) | copy-start | bytes 6291460
  75.8 6.4 %copy-start.8 = (bf16[4,128,64,16]{1,0,3,2:T(4,128)(2,1)}, bf16[4,128,64,16]{1,0,3,2:T(4,128)(2,1)S(1)}, u32[]{:S(2)}) copy-start(bf16[4,128,64,16]{1,0,3,2:T(4,128)(2,1)S(1)} %reshape.116) | copy-start | bytes 3145732
  79.7 2.8 copy-start.2
  199.3 8.7 %copy-start.16 = (bf16[512,1024]{1,0:T(8,128)(2,1)S(1)}, bf16[512,1024]{1,0:T(8,128)(2,1)}, u32[]{:S(2)}) copy-start(bf16[512,1024]{1,0:T(8,128)(2,1)} %convolution_convert_fusion.1) | copy-start | bytes 3145732
  207.9 8.3 %copy-start.28 = (bf16[512,4096]{1,0:T(8,128)(2,1)S(1)}, bf16[512,4096]{1,0:T(8,128)(2,1)}, u32[]{:S(2)}) copy-start(bf16[512,4096]{1,0:T(8,128)(2,1)} %all-gather.3.cloned.1.call-done) | copy-start | bytes 12582916
  223.3 195.4 %reduce-scatter.3.cloned.1.call-start = ((), (), s32[]{:S(2)}) async-start(), calls=%async_computation.9 | async-start | bytes 5242880 | tf_op jit(solution)/shard_map/reduce_scatter | solution.py:226
  232.8 1.6 copy-start.12
  238.6 4.4 %copy-start.11 = (bf16[128,4,1024]{0,2,1:T(8,128)(2,1)S(1)}, bf16[128,4,1024]{0,2,1:T(8,128)(2,1)}, u32[]{:S(2)}) copy-start(bf16[128,4,1024]{0,2,1:T(8,128)(2,1)} %copy-done.10) | copy-start | bytes 3145732
  239.7 3.4 copy-start.3
  243.0 4.5 %copy-start.13 = (f32[512,1024]{0,1:T(8,128)S(1)}, f32[512,1024]{0,1:T(8,128)}, u32[]{:S(2)}) copy-start(f32[512,1024]{0,1:T(8,128)} %get-tuple-element.56) | copy-start | bytes 6291460
  246.5 1.7 copy-start.5
  246.5 2.0 copy-start.7
  253.7 7.3 %copy-start.9 = (bf16[4,128,64,16]{1,0,3,2:T(4,128)(2,1)S(1)}, bf16[4,128,64,16]{1,0,3,2:T(4,128)(2,1)}, u32[]{:S(2)}) copy-start(bf16[4,128,64,16]{1,0,3,2:T(4,128)(2,1)} %copy-done.8) | copy-start | bytes 3145732
  254.7 82.8 %collective-permute-start = (bf16[128,1024]{0,1:T(8,128)(2,1)}, bf16[128,1024]{0,1:T(8,128)(2,1)}, u32[]{:S(2)}, u32[]{:S(2)}) collective-permute-start(bf16[128,1024]{0,1:T(8,128)(2,1)} %get-tuple-element.62), channel_id=1, source_target_pairs={{0,1},{1,0},{2,3},{3,2},{4,5},{5,4},{6,7},{7,6},{8,9},{9,8},{10,11... | collective-permute-start | bytes 786440 | tf_op jit(solution)/shard_map/ppermute | solution.py:19
  254.7 83.9 %collective-permute-start.1 = (bf16[128,1024]{0,1:T(8,128)(2,1)}, bf16[128,1024]{0,1:T(8,128)(2,1)}, u32[]{:S(2)}, u32[]{:S(2)}) collective-permute-start(bf16[128,1024]{0,1:T(8,128)(2,1)} %get-tuple-element.61), channel_id=1, source_target_pairs={{0,2},{1,3},{2,0},{3,1},{4,6},{5,7},{6,4},{7,5},{8,10},{9,11},{10,... | collective-permute-start | bytes 786440 | tf_op jit(solution)/shard_map/ppermute | solution.py:19
  256.2 83.5 %collective-permute-start.2 = (bf16[128,1024]{0,1:T(8,128)(2,1)}, bf16[128,1024]{0,1:T(8,128)(2,1)}, u32[]{:S(2)}, u32[]{:S(2)}) collective-permute-start(bf16[128,1024]{0,1:T(8,128)(2,1)} %get-tuple-element.60), channel_id=1, source_target_pairs={{0,3},{1,2},{2,1},{3,0},{4,7},{5,6},{6,5},{7,4},{8,11},{9,10},{10,... | collective-permute-start | bytes 786440 | tf_op jit(solution)/shard_map/ppermute | solution.py:19
  256.5 40.3 %all-to-all-start.3 = ((bf16[4,128,1024]{2,1,0:T(8,128)(2,1)}), bf16[4,128,1024]{2,1,0:T(8,128)(2,1)}, u32[]{:S(2)}, u32[]{:S(2)}) async-start(bf16[4,128,1024]{2,1,0:T(8,128)(2,1)} %bitcast.173), calls=%async_computation.4 | async-start | bytes 2097152 | tf_op jit(solution)/shard_map/all_to_all | solution.py:200
  285.1 6.5 %copy-start.14 = (f32[512,1024]{0,1:T(8,128)S(1)}, f32[512,1024]{0,1:T(8,128)}, u32[]{:S(2)}) copy-start(f32[512,1024]{0,1:T(8,128)} %get-tuple-element.52) | copy-start | bytes 6291460
  296.8 3.9 copy-start.22
  296.8 3.9 copy-start.23
  296.8 3.9 copy-start.24
  296.8 3.9 copy-start.25
  296.8 3.9 copy-start.26
  296.8 3.9 copy-start.27
  296.8 4.0 copy-start.21
  296.8 46.7 %all-to-all-start.4 = ((bf16[4,128,1024]{1,2,0:T(8,128)(2,1)}), bf16[4,128,1024]{1,2,0:T(8,128)(2,1)S(1)}, u32[]{:S(2)}, u32[]{:S(2)}) async-start(bf16[4,128,1024]{1,2,0:T(8,128)(2,1)} %copy_bitcast_fusion.2), calls=%async_computation.5 | async-start | bytes 2097152 | tf_op jit(solution)/shard_map/all_to_all | solution.py:203
  340.9 4.0 copy-start.20
  343.6 75.1 %copy-start.1 = (bf16[128,256]{1,0:T(8,128)(2,1)S(1)}, bf16[128,256]{1,0:T(8,128)(2,1)}, u32[]{:S(2)}) copy-start(bf16[128,256]{1,0:T(8,128)(2,1)} %param.12) | copy-start | bytes 196612
Sparse Core Ops, SparseCore 0:
  9.6 52.1 all-gather.2
  63.9 125.1 all-gather.4
  223.4 148.6 reduce-scatter.4
  375.2 43.4 reduce-scatter.2
